TPU v7x, 32 devices: a whole 2x2x4 slice. The times are simulated.
32 devices in a mesh: samp: 4 (over y, x), var: 8 (over z, core).
Axes of the slice: x: 2, y: 2, z: 4, core: 2. Of those that a mesh axis runs over, the one named last changes fastest.
Arguments:
- dosage: bfloat16 [8192, 16384], P('samp', 'var'), may hold values from -6 to 6
- traits: float32 [8192, 128], P(('samp', 'var')), may hold values from -6 to 6
- coef_now: float32 [128, 256, 128], P('var', 'samp'), may hold values from -6 to 6
- coef_prev: float32 [128, 256, 128], P('var', 'samp'), may hold values from -6 to 6
- block_inverse: bfloat16 [128, 256, 4, 256], P('var', 'samp'), may hold values from -0.1875 to 0.1875
- penalty: float32 [128], replicated, may hold values from 0.05 to 0.5
- block_start: int32 [64], replicated, may hold values from 0 to 1, as said below
- unit_owner: int32 [64], replicated, may hold values from 0 to 7, as said below
Outputs:
- coef_next: float32 [128, 256, 128], P('var', 'samp')
- residual: float32 [8192, 128], P(('samp', 'var'))
Inputs may be any that keep to these rules, and one draw needn't show every extreme that they name: `block_start`: 1 where a linkage block begins, else 0. The first unit of every device's 8 units begins a block, and a block holds 1 to 4 units of 256 variants. `unit_owner`: the index along var of the device that owns each unit's block, equal for all units of a block. For a unit of the device with index d along var it is (d + j) modulo the size of var, with 1 <= j <= 4. An owner holds at most 16 units and some owner holds exactly 16; the units of one device that belong to one owner are at most 4, and some device has exactly 4 for one owner.
All inputs are finite; a program needn't handle non-finite values.
Results may differ from a plain program's by a relative error of at most 0.0072.
Values may be sent and summed in bfloat16 or wider, within the bound.
No kernel may reach another device: no remote copies, remote signals or barrier semaphores. Data moves between devices by JAX's collectives and lax.ppermute only.
A program may use at most 64 MiB of HBM per device.

v0:
```python
import math
import jax
import jax.numpy as jnp
from jax import lax
from jax.sharding import PartitionSpec as P

MOMENTA = (0.4, 0.55)


def shifted(block, axis, distance):
    devices = range(lax.axis_size(axis))
    route = [((i - distance) % len(devices), i) for i in devices]
    return lax.ppermute(block, axis, route)


def unit_tables(block_start, unit_owner, per_device, owners):
    unit_count = block_start.shape[0]
    unit_ids = jnp.arange(unit_count, dtype=jnp.int32)
    shard_of = unit_ids // per_device
    owner_hot = (unit_owner[:, None] == jnp.arange(owners, dtype=jnp.int32)[None, :]).astype(
        jnp.int32
    )
    running = jnp.cumsum(owner_hot, axis=0) - owner_hot
    slot_index = jnp.sum(running * owner_hot, axis=1)
    first_unit = shard_of * per_device
    before_shard = jnp.sum(running[first_unit] * owner_hot, axis=1)
    pair_place = slot_index - before_shard
    block_begin = lax.cummax(jnp.where(block_start == 1, unit_ids, 0), axis=0)
    block_later = lax.cummin(
        jnp.where(block_start == 1, unit_ids, unit_count), axis=0, reverse=True
    )
    block_follow = jnp.concatenate([block_later[1:], jnp.full((1,), unit_count, jnp.int32)])
    block_length = block_follow - block_begin
    offset = unit_ids - block_begin
    return (shard_of, slot_index, pair_place, offset, block_length)


def shards(dosage, traits, coef_now, coef_prev, block_inverse, penalty, block_start, unit_owner):
    owners = lax.axis_size("var")
    quarters = lax.axis_size("samp")
    var_index = lax.axis_index("var")
    samp_index = lax.axis_index("samp")
    capacity = coef_now.shape[0]
    quarter_rows = coef_now.shape[1]
    right_cols = coef_now.shape[2]
    unit_rows = block_inverse.shape[3]
    block_most = block_inverse.shape[2]
    per_device = dosage.shape[1] // unit_rows
    pair_cap = min(block_most, per_device)
    reach = capacity // pair_cap
    samples = dosage.shape[0] * quarters
    variants = dosage.shape[1] * owners
    inv_scale = 1.0 / math.sqrt(variants)
    grad_scale = 0.5 / math.sqrt(samples)
    shard_of, slot_index, pair_place, offset, block_length = unit_tables(
        block_start, unit_owner, per_device, owners
    )
    owner_gap = (unit_owner - shard_of) % owners
    unit_code = (owner_gap - 1) * pair_cap + pair_place
    columns = jnp.arange(reach * pair_cap, dtype=jnp.int32)
    local_ids = var_index * per_device + jnp.arange(per_device, dtype=jnp.int32)
    local_code = unit_code[local_ids]
    matches = local_code[None, :] == columns[:, None]
    send_unit = jnp.sum(
        matches.astype(jnp.int32) * jnp.arange(per_device, dtype=jnp.int32)[None, :], axis=1
    )
    send_live = jnp.any(matches, axis=1)
    owned_flag = unit_owner == var_index
    slot_match = owned_flag[None, :] & (
        slot_index[None, :] == jnp.arange(capacity, dtype=jnp.int32)[:, None]
    )
    slot_hits = slot_match.astype(jnp.int32)
    slot_live = jnp.any(slot_match, axis=1)
    slot_code = jnp.sum(slot_hits * unit_code[None, :], axis=1)
    slot_offset = jnp.sum(slot_hits * offset[None, :], axis=1)
    slot_length = jnp.sum(slot_hits * block_length[None, :], axis=1)
    back_match = slot_live[None, :] & (slot_code[None, :] == columns[:, None])
    back_slot = jnp.sum(
        back_match.astype(jnp.int32) * jnp.arange(capacity, dtype=jnp.int32)[None, :], axis=1
    )
    back_live = jnp.any(back_match, axis=1)
    within = jnp.arange(block_most, dtype=jnp.int32)
    member_ids = jnp.clip(
        jnp.arange(capacity, dtype=jnp.int32)[:, None] - slot_offset[:, None] + within[None, :],
        0,
        capacity - 1,
    )
    member_live = (within[None, :] < slot_length[:, None]) & slot_live[:, None]
    panel_rows = block_inverse.reshape(capacity, quarter_rows, block_most * unit_rows)
    zero_half = jnp.zeros((), jnp.bfloat16)
    current, previous = (coef_now, coef_prev)
    residual = traits
    for momentum in MOMENTA:
        point = current + momentum * (current - previous)
        send_outgoing = jnp.where(
            back_live[:, None, None], point.astype(jnp.bfloat16)[back_slot], zero_half
        )
        send_outgoing = send_outgoing.reshape(reach, pair_cap, quarter_rows, right_cols)
        send_pieces = []
        for send_gap in range(1, reach + 1):
            send_pieces.append(shifted(send_outgoing[send_gap - 1], "var", -send_gap))
        send_received = jnp.stack(send_pieces).reshape(reach * pair_cap, quarter_rows, right_cols)
        local_rows = send_received[local_code]
        send_gathered = lax.all_gather(local_rows[:, None], "samp", axis=1, tiled=True)
        values = send_gathered.reshape(per_device * unit_rows, right_cols)
        summed = lax.psum_scatter(
            jnp.dot(dosage, values, preferred_element_type=jnp.float32) * inv_scale,
            "var",
            scatter_dimension=0,
            tiled=True,
        )
        residual = summed - traits
        residual_b = lax.all_gather(residual.astype(jnp.bfloat16), "var", axis=0, tiled=True)
        partial_grad = (
            lax.dot_general(
                dosage, residual_b, (((0,), (0,)), ((), ())), preferred_element_type=jnp.float32
            )
            * grad_scale
        )
        shaped = partial_grad.reshape(per_device, quarters, quarter_rows, right_cols)
        grad_sum = lax.psum(shaped, "samp")
        own_grad = lax.dynamic_index_in_dim(grad_sum, samp_index, 1, keepdims=False)
        outgoing = jnp.where(
            send_live[:, None, None], own_grad.astype(jnp.bfloat16)[send_unit], zero_half
        )
        outgoing = outgoing.reshape(reach, pair_cap, quarter_rows, right_cols)
        pieces = []
        for gap in range(1, reach + 1):
            pieces.append(shifted(outgoing[gap - 1], "var", gap))
        received = jnp.stack(pieces).reshape(reach * pair_cap, quarter_rows, right_cols)
        held_rows = jnp.where(slot_live[:, None, None], received[slot_code], zero_half)
        gathered = lax.all_gather(held_rows[:, None], "samp", axis=1, tiled=True)
        whole_grad = gathered.reshape(capacity, unit_rows, right_cols)
        block_grad = jnp.where(member_live[:, :, None, None], whole_grad[member_ids], zero_half)
        block_grad = block_grad.reshape(capacity, block_most * unit_rows, right_cols)
        direction = jnp.einsum(
            "irc,ick->irk", panel_rows, block_grad, preferred_element_type=jnp.float32
        )
        stepped = point - direction
        updated = jnp.sign(stepped) * jnp.maximum(jnp.abs(stepped) - penalty, 0.0)
        updated = jnp.where(slot_live[:, None, None], updated, jnp.float32(0.0))
        previous, current = (current, updated)
    return (current, residual)


def solution(mesh):
    placed = (
        P("samp", "var"),
        P(("samp", "var"), None),
        P("var", "samp", None),
        P("var", "samp", None),
        P("var", "samp", None, None),
        P(),
        P(),
        P(),
    )
    return jax.shard_map(
        shards,
        mesh=mesh,
        in_specs=placed,
        out_specs=(P("var", "samp", None), P(("samp", "var"), None)),
        check_vma=False,
    )
```

profile of v0, /device:TPU:0, one launch (start us, length us, event | category | flops | bytes accessed | tf_op | source)
XLA Modules:
  0.0 374.6 jit_solution(17077146969779160908)
XLA Ops:
  7.2 0.7 fusion.9
  8.0 0.7 broadcast_compare_fusion
  8.6 0.7 fusion.20
  9.4 0.6 reduce-window.12
  10.5 0.7 fusion.10
  11.2 0.6 gather_fusion
  11.8 0.8 select_reduce_fusion
  12.8 0.7 iota_subtract_fusion
  13.5 0.1 select_reduce_fusion.5
  13.8 0.1 select_reduce_fusion.3
  13.9 1.3 fusion.6
  15.2 0.6 gather_fusion.2
  15.9 4.6 %collective-permute-start = (bf16[4,64,128]{2,1,0:T(8,128)(2,1)S(1)}, bf16[4,64,128]{2,1,0:T(8,128)(2,1)S(1)}, u32[]{:S(2)}, u32[]{:S(2)}) collective-permute-start(bf16[4,64,128]{2,1,0:T(8,128)(2,1)S(1)} %get-tuple-element.27), channel_id=1, source_target_pairs={{1,0},{2,1},{3,2},{4,3},{5,4},{6,5},{7,6},{0,7},{9,8},{10,9},{11,1... | collective-permute-start | bytes 196616 | tf_op jit(solution)/shard_map/ppermute | solution.py:13
  20.5 3.3 collective-permute-start.1
  23.8 0.6 gather_fusion.1
  24.5 2.6 collective-permute-done.3
  27.1 0.6 gather_fusion.3
  27.7 11.3 %all-gather = bf16[8,256,128]{2,1,0:T(8,128)(2,1)S(1)} all-gather(bf16[8,64,128]{2,1,0:T(8,128)(2,1)S(1)} %gather_fusion.3), channel_id=2, replica_groups=mesh['samp'=4,'var'=8] {'samp'}, dimensions={1}, use_global_device_ids=true | all-gather | bytes 655360 | tf_op jit(solution)/shard_map/all_gather | solution.py:104
  39.0 7.4 %fusion.3 = f32[2048,128]{0,1:T(8,128)} fusion(bf16[2048,128]{1,0:T(8,128)(2,1)S(1)} %bitcast.106, bf16[2048,2048]{1,0:T(8,128)(2,1)} %param.8), kind=kOutput, calls=%fused_computation.21 | convolution fusion | flops 1074003968 | bytes 9961472 | tf_op jit(solution)/shard_map/dot_general | solution.py:107
  46.8 32.6 %reduce-scatter.3.cloned.1.call-done = f32[256,128]{0,1:T(8,128)} async-done(((f32[2048,128]{0,1:T(8,128)}), f32[256,128]{0,1:T(8,128)}) %reduce-scatter.3.cloned.1.call-update) | async-done | bytes 131088 | tf_op jit(solution)/shard_map/reduce_scatter | solution.py:106
  79.4 0.9 subtract_convert_fusion
  80.3 14.9 %all_gather.19 = bf16[2048,128]{0,1:T(8,128)(2,1)S(1)} all-gather(bf16[256,128]{0,1:T(8,128)(2,1)S(1)} %subtract_convert_fusion), channel_id=1, replica_groups=mesh['samp'=4,'var'=8] {'var'}, dimensions={0}, use_global_device_ids=true | all-gather | bytes 589824 | tf_op jit(solution)/shard_map/all_gather | solution.py:113
  95.3 4.7 %fusion.2 = f32[2048,128]{0,1:T(8,128)S(1)} fusion(bf16[2048,128]{0,1:T(8,128)(2,1)S(1)} %all_gather.19, bf16[2048,2048]{1,0:T(8,128)(2,1)} %param.8), kind=kOutput, calls=%fused_computation.19 | convolution fusion | flops 1074003968 | bytes 9961472 | tf_op jit(solution)/shard_map/dot_general | solution.py:115
  100.0 0.3 copy.25
  100.3 41.9 %all-reduce.2 = bf16[8,4,64,128]{3,2,1,0:T(8,128)(2,1)S(1)} all-reduce(f32[8,4,64,128]{3,2,1,0:T(8,128)S(1)} %bitcast.104), channel_id=1, replica_groups=mesh['samp'=4,'var'=8] {'samp'}, use_global_device_ids=true, to_apply=%region_12.13 | all-reduce | flops 262144 | bytes 1572864 | tf_op jit(solution)/shard_map/psum | solution.py:121
  142.3 0.6 gather_fusion.4
  143.1 0.7 collective-permute-start.7
  143.8 3.1 collective-permute-start.6
  146.9 1.7 collective-permute-done.4
  148.6 4.5 %collective-permute-done.7 = bf16[4,64,128]{2,1,0:T(8,128)(2,1)S(1)} collective-permute-done((bf16[4,64,128]{2,1,0:T(8,128)(2,1)S(1)}, bf16[4,64,128]{2,1,0:T(8,128)(2,1)S(1)}, u32[]{:S(2)}, u32[]{:S(2)}) %collective-permute-start.7) | collective-permute-done | bytes 65568 | tf_op jit(solution)/shard_map/ppermute | solution.py:13
  153.2 0.6 gather_fusion.5
  153.8 0.8 bitcast_select_fusion.3
  155.1 3.2 reshape.362
  158.3 20.1 %all-gather.5.cloned.1.call-done = bf16[16,4,64,128]{3,2,1,0:T(8,128)(2,1)} async-done(((bf16[16,1,64,128]{3,2,1,0:T(8,128)(2,1)}), bf16[16,4,64,128]{3,2,1,0:T(8,128)(2,1)}) %all-gather.5.cloned.1.call-update) | async-done | bytes 1048592 | tf_op jit(solution)/shard_map/all_gather | solution.py:132
  178.5 4.2 %gather_fusion.6 = bf16[64,256,128]{2,1,0:T(8,128)(2,1)} fusion(bf16[16,256,128]{2,1,0:T(8,128)(2,1)} %bitcast.100, s32[1024]{0:T(1024)S(1)} %pad_clamp_fusion), kind=kCustom, calls=%fused_computation.6 | custom fusion | bytes 8388864 | tf_op jit(solution)/shard_map/gather | solution.py:134
  182.7 6.2 %bitcast_select_fusion.1 = bf16[16,1024,128]{2,1,0:T(8,128)(2,1)S(1)} fusion(pred[16,1024]{1,0:T(8,128)(4,1)S(1)} %bitcast.112, bf16[16,1024,128]{2,1,0:T(8,128)(2,1)} %bitcast.103), kind=kLoop, calls=%fused_computation.13 | loop fusion | flops 2097152 | bytes 8404992 | tf_op jit(solution)/shard_map/jit(_where)/select_n | solution.py:134
  188.9 1.8 fusion.36
  190.7 0.6 gather_fusion.7
  191.5 2.7 collective-permute-start.8
  194.1 0.2 collective-permute-start.10
  194.3 3.3 collective-permute-start.9
  197.6 3.1 collective-permute-done.11
  200.7 0.6 gather_fusion.8
  201.3 11.5 %all-gather.1 = bf16[8,256,128]{2,1,0:T(8,128)(2,1)S(1)} all-gather(bf16[8,64,128]{2,1,0:T(8,128)(2,1)S(1)} %gather_fusion.8), channel_id=3, replica_groups=mesh['samp'=4,'var'=8] {'samp'}, dimensions={1}, use_global_device_ids=true | all-gather | bytes 655360 | tf_op jit(solution)/shard_map/all_gather | solution.py:104
  212.9 7.3 %fusion.1 = f32[2048,128]{0,1:T(8,128)} fusion(bf16[2048,128]{1,0:T(8,128)(2,1)S(1)} %bitcast.107, bf16[2048,2048]{1,0:T(8,128)(2,1)} %param.8), kind=kOutput, calls=%fused_computation.17 | convolution fusion | flops 1074003968 | bytes 9961472 | tf_op jit(solution)/shard_map/dot_general | solution.py:107
  220.2 33.1 %reduce-scatter.5.cloned.1.call-done = f32[256,128]{0,1:T(8,128)} async-done(((f32[2048,128]{0,1:T(8,128)}), f32[256,128]{0,1:T(8,128)}) %reduce-scatter.5.cloned.1.call-update) | async-done | bytes 131088 | tf_op jit(solution)/shard_map/reduce_scatter | solution.py:106
  253.3 0.9 fusion.31
  254.2 14.9 %all_gather.22 = bf16[2048,128]{0,1:T(8,128)(2,1)S(1)} all-gather(bf16[256,128]{0,1:T(8,128)(2,1)S(1)} %get-tuple-element.13), channel_id=1, replica_groups=mesh['samp'=4,'var'=8] {'var'}, dimensions={0}, use_global_device_ids=true | all-gather | bytes 589824 | tf_op jit(solution)/shard_map/all_gather | solution.py:113
  269.2 5.7 %fusion = f32[2048,128]{0,1:T(8,128)} fusion(bf16[2048,128]{0,1:T(8,128)(2,1)S(1)} %all_gather.22, bf16[2048,2048]{1,0:T(8,128)(2,1)} %param.8), kind=kOutput, calls=%fused_computation.15 | convolution fusion | flops 1074003968 | bytes 9961472 | tf_op jit(solution)/shard_map/dot_general | solution.py:115
  274.9 1.5 copy.27
  276.4 42.3 %all-reduce.3 = bf16[8,4,64,128]{3,2,1,0:T(8,128)(2,1)} all-reduce(f32[8,4,64,128]{3,2,1,0:T(8,128)S(1)} %bitcast.105), channel_id=1, replica_groups=mesh['samp'=4,'var'=8] {'samp'}, use_global_device_ids=true, to_apply=%region_16.17 | all-reduce | flops 262144 | bytes 1572864 | tf_op jit(solution)/shard_map/psum | solution.py:121
  318.8 0.9 fusion.8
  319.7 0.6 gather_fusion.9
  320.5 0.7 collective-permute-start.15
  321.2 3.1 collective-permute-start.14
  324.3 1.8 collective-permute-done.12
  326.0 4.5 %collective-permute-done.15 = bf16[4,64,128]{2,1,0:T(8,128)(2,1)S(1)} collective-permute-done((bf16[4,64,128]{2,1,0:T(8,128)(2,1)S(1)}, bf16[4,64,128]{2,1,0:T(8,128)(2,1)S(1)}, u32[]{:S(2)}, u32[]{:S(2)}) %collective-permute-start.15) | collective-permute-done | bytes 65568 | tf_op jit(solution)/shard_map/ppermute | solution.py:13
  330.7 0.6 gather_fusion.10
  331.3 0.8 bitcast_select_fusion.2
  332.1 0.8 copy.28
  332.8 23.1 %all-gather.7.cloned.1.call-done = bf16[16,4,64,128]{3,2,1,0:T(8,128)(2,1)} async-done(((bf16[16,1,64,128]{3,2,1,0:T(8,128)(2,1)}), bf16[16,4,64,128]{3,2,1,0:T(8,128)(2,1)}) %all-gather.7.cloned.1.call-update) | async-done | bytes 1048592 | tf_op jit(solution)/shard_map/all_gather | solution.py:132
  355.9 4.2 %gather_fusion.11 = bf16[64,256,128]{2,1,0:T(8,128)(2,1)} fusion(bf16[16,256,128]{2,1,0:T(8,128)(2,1)} %bitcast.101, s32[1024]{0:T(1024)S(1)} %pad_clamp_fusion), kind=kCustom, calls=%fused_computation.11 | custom fusion | bytes 8388864 | tf_op jit(solution)/shard_map/gather | solution.py:134
  360.1 6.1 %bitcast_select_fusion = bf16[16,1024,128]{2,1,0:T(8,128)(2,1)S(1)} fusion(pred[16,1024]{1,0:T(8,128)(4,1)S(1)} %bitcast.113, bf16[16,1024,128]{2,1,0:T(8,128)(2,1)} %bitcast.102), kind=kLoop, calls=%fused_computation.12 | loop fusion | flops 2097152 | bytes 8404992 | tf_op jit(solution)/shard_map/jit(_where)/select_n | solution.py:134
  366.3 1.8 multiply_select_fusion
  (78 shorter events, 2.7 us)
Async XLA Ops:
  7.2 72.2 %reduce-scatter.3.cloned.1.call-start = ((), (), s32[]{:S(2)}) async-start(), calls=%async_computation.2 | async-start | bytes 1179648 | tf_op jit(solution)/shard_map/reduce_scatter | solution.py:106
  15.9 8.6 %collective-permute-start = (bf16[4,64,128]{2,1,0:T(8,128)(2,1)S(1)}, bf16[4,64,128]{2,1,0:T(8,128)(2,1)S(1)}, u32[]{:S(2)}, u32[]{:S(2)}) collective-permute-start(bf16[4,64,128]{2,1,0:T(8,128)(2,1)S(1)} %get-tuple-element.27), channel_id=1, source_target_pairs={{1,0},{2,1},{3,2},{4,3},{5,4},{6,5},{7,6},{0,7},{9,8},{10,9},{11,1... | collective-permute-start | bytes 196616 | tf_op jit(solution)/shard_map/ppermute | solution.py:13
  20.5 6.6 %collective-permute-start.3 = (bf16[4,64,128]{2,1,0:T(8,128)(2,1)S(1)}, bf16[4,64,128]{2,1,0:T(8,128)(2,1)S(1)}, u32[]{:S(2)}, u32[]{:S(2)}) collective-permute-start(bf16[4,64,128]{2,1,0:T(8,128)(2,1)S(1)} %get-tuple-element.28), channel_id=1, source_target_pairs={{4,0},{5,1},{6,2},{7,3},{0,4},{1,5},{2,6},{3,7},{12,8},{13,9},{14,... | collective-permute-start | bytes 196616 | tf_op jit(solution)/shard_map/ppermute | solution.py:13
  20.5 6.6 %collective-permute-start.2 = (bf16[4,64,128]{2,1,0:T(8,128)(2,1)S(1)}, bf16[4,64,128]{2,1,0:T(8,128)(2,1)S(1)}, u32[]{:S(2)}, u32[]{:S(2)}) collective-permute-start(bf16[4,64,128]{2,1,0:T(8,128)(2,1)S(1)} %get-tuple-element.29), channel_id=1, source_target_pairs={{3,0},{4,1},{5,2},{6,3},{7,4},{0,5},{1,6},{2,7},{11,8},{12,9},{13,... | collective-permute-start | bytes 196616 | tf_op jit(solution)/shard_map/ppermute | solution.py:13
  20.5 6.6 %collective-permute-start.1 = (bf16[4,64,128]{2,1,0:T(8,128)(2,1)S(1)}, bf16[4,64,128]{2,1,0:T(8,128)(2,1)S(1)}, u32[]{:S(2)}, u32[]{:S(2)}) collective-permute-start(bf16[4,64,128]{2,1,0:T(8,128)(2,1)S(1)} %get-tuple-element.30), channel_id=1, source_target_pairs={{2,0},{3,1},{4,2},{5,3},{6,4},{7,5},{0,6},{1,7},{10,8},{11,9},{12,... | collective-permute-start | bytes 196616 | tf_op jit(solution)/shard_map/ppermute | solution.py:13
  39.0 7.4 %copy-start.3 = (f32[256,128]{1,0:T(8,128)S(1)}, f32[256,128]{1,0:T(8,128)}, u32[]{:S(2)}) copy-start(f32[256,128]{1,0:T(8,128)} %param.9) | copy-start | bytes 393220
  46.4 132.1 %all-gather.5.cloned.1.call-start = ((), (), s32[]{:S(2)}) async-start(), calls=%async_computation.3 | async-start | bytes 1310720 | tf_op jit(solution)/shard_map/all_gather | solution.py:132
  143.0 5.6 %collective-permute-start.4 = (bf16[4,64,128]{2,1,0:T(8,128)(2,1)S(1)}, bf16[4,64,128]{2,1,0:T(8,128)(2,1)S(1)}, u32[]{:S(2)}, u32[]{:S(2)}) collective-permute-start(bf16[4,64,128]{2,1,0:T(8,128)(2,1)S(1)} %get-tuple-element.23), channel_id=1, source_target_pairs={{7,0},{0,1},{1,2},{2,3},{3,4},{4,5},{5,6},{6,7},{15,8},{8,9},{9,10... | collective-permute-start | bytes 196616 | tf_op jit(solution)/shard_map/ppermute | solution.py:13
  143.1 10.1 %collective-permute-start.7 = (bf16[4,64,128]{2,1,0:T(8,128)(2,1)S(1)}, bf16[4,64,128]{2,1,0:T(8,128)(2,1)S(1)}, u32[]{:S(2)}, u32[]{:S(2)}) collective-permute-start(bf16[4,64,128]{2,1,0:T(8,128)(2,1)S(1)} %get-tuple-element.24), channel_id=1, source_target_pairs={{4,0},{5,1},{6,2},{7,3},{0,4},{1,5},{2,6},{3,7},{12,8},{13,9},{14,... | collective-permute-start | bytes 196616 | tf_op jit(solution)/shard_map/ppermute | solution.py:13
  143.8 9.4 %collective-permute-start.6 = (bf16[4,64,128]{2,1,0:T(8,128)(2,1)S(1)}, bf16[4,64,128]{2,1,0:T(8,128)(2,1)S(1)}, u32[]{:S(2)}, u32[]{:S(2)}) collective-permute-start(bf16[4,64,128]{2,1,0:T(8,128)(2,1)S(1)} %get-tuple-element.25), channel_id=1, source_target_pairs={{5,0},{6,1},{7,2},{0,3},{1,4},{2,5},{3,6},{4,7},{13,8},{14,9},{15,... | collective-permute-start | bytes 196616 | tf_op jit(solution)/shard_map/ppermute | solution.py:13
  146.9 6.3 %collective-permute-start.5 = (bf16[4,64,128]{2,1,0:T(8,128)(2,1)S(1)}, bf16[4,64,128]{2,1,0:T(8,128)(2,1)S(1)}, u32[]{:S(2)}, u32[]{:S(2)}) collective-permute-start(bf16[4,64,128]{2,1,0:T(8,128)(2,1)S(1)} %get-tuple-element.26), channel_id=1, source_target_pairs={{6,0},{7,1},{0,2},{1,3},{2,4},{3,5},{4,6},{5,7},{14,8},{15,9},{8,1... | collective-permute-start | bytes 196616 | tf_op jit(solution)/shard_map/ppermute | solution.py:13
  154.7 98.7 %reduce-scatter.5.cloned.1.call-start = ((), (), s32[]{:S(2)}) async-start(), calls=%async_computation.4 | async-start | bytes 1179648 | tf_op jit(solution)/shard_map/reduce_scatter | solution.py:106
  182.7 6.2 %copy-start = (f32[16,64,128]{2,1,0:T(8,128)S(1)}, f32[16,64,128]{2,1,0:T(8,128)}, u32[]{:S(2)}) copy-start(f32[16,64,128]{2,1,0:T(8,128)} %param.10) | copy-start | bytes 1572868
  182.7 6.2 %copy-start.1 = (f32[16,64,128]{2,1,0:T(8,128)S(1)}, f32[16,64,128]{2,1,0:T(8,128)}, u32[]{:S(2)}) copy-start(f32[16,64,128]{2,1,0:T(8,128)} %param.11) | copy-start | bytes 1572868
  182.7 6.2 %copy-start.4 = (f32[128]{0:T(128)S(1)}, f32[128]{0:T(128)}, u32[]{:S(2)}) copy-start(f32[128]{0:T(128)} %param.13) | copy-start | bytes 1540
  191.5 6.1 %collective-permute-start.8 = (bf16[4,64,128]{2,1,0:T(8,128)(2,1)S(1)}, bf16[4,64,128]{2,1,0:T(8,128)(2,1)S(1)}, u32[]{:S(2)}, u32[]{:S(2)}) collective-permute-start(bf16[4,64,128]{2,1,0:T(8,128)(2,1)S(1)} %get-tuple-element.19), channel_id=1, source_target_pairs={{1,0},{2,1},{3,2},{4,3},{5,4},{6,5},{7,6},{0,7},{9,8},{10,9},{11,1... | collective-permute-start | bytes 196616 | tf_op jit(solution)/shard_map/ppermute | solution.py:13
  194.1 6.6 %collective-permute-start.11 = (bf16[4,64,128]{2,1,0:T(8,128)(2,1)S(1)}, bf16[4,64,128]{2,1,0:T(8,128)(2,1)S(1)}, u32[]{:S(2)}, u32[]{:S(2)}) collective-permute-start(bf16[4,64,128]{2,1,0:T(8,128)(2,1)S(1)} %get-tuple-element.20), channel_id=1, source_target_pairs={{4,0},{5,1},{6,2},{7,3},{0,4},{1,5},{2,6},{3,7},{12,8},{13,9},{14,... | collective-permute-start | bytes 196616 | tf_op jit(solution)/shard_map/ppermute | solution.py:13
  194.1 6.6 %collective-permute-start.10 = (bf16[4,64,128]{2,1,0:T(8,128)(2,1)S(1)}, bf16[4,64,128]{2,1,0:T(8,128)(2,1)S(1)}, u32[]{:S(2)}, u32[]{:S(2)}) collective-permute-start(bf16[4,64,128]{2,1,0:T(8,128)(2,1)S(1)} %get-tuple-element.21), channel_id=1, source_target_pairs={{3,0},{4,1},{5,2},{6,3},{7,4},{0,5},{1,6},{2,7},{11,8},{12,9},{13,... | collective-permute-start | bytes 196616 | tf_op jit(solution)/shard_map/ppermute | solution.py:13
  194.3 6.4 %collective-permute-start.9 = (bf16[4,64,128]{2,1,0:T(8,128)(2,1)S(1)}, bf16[4,64,128]{2,1,0:T(8,128)(2,1)S(1)}, u32[]{:S(2)}, u32[]{:S(2)}) collective-permute-start(bf16[4,64,128]{2,1,0:T(8,128)(2,1)S(1)} %get-tuple-element.22), channel_id=1, source_target_pairs={{2,0},{3,1},{4,2},{5,3},{6,4},{7,5},{0,6},{1,7},{10,8},{11,9},{12,... | collective-permute-start | bytes 196616 | tf_op jit(solution)/shard_map/ppermute | solution.py:13
  220.2 135.7 %all-gather.7.cloned.1.call-start = ((), (), s32[]{:S(2)}) async-start(), calls=%async_computation.5 | async-start | bytes 1310720 | tf_op jit(solution)/shard_map/all_gather | solution.py:132
  320.4 5.6 %collective-permute-start.12 = (bf16[4,64,128]{2,1,0:T(8,128)(2,1)S(1)}, bf16[4,64,128]{2,1,0:T(8,128)(2,1)S(1)}, u32[]{:S(2)}, u32[]{:S(2)}) collective-permute-start(bf16[4,64,128]{2,1,0:T(8,128)(2,1)S(1)} %get-tuple-element.15), channel_id=1, source_target_pairs={{7,0},{0,1},{1,2},{2,3},{3,4},{4,5},{5,6},{6,7},{15,8},{8,9},{9,10... | collective-permute-start | bytes 196616 | tf_op jit(solution)/shard_map/ppermute | solution.py:13
  320.5 10.1 %collective-permute-start.15 = (bf16[4,64,128]{2,1,0:T(8,128)(2,1)S(1)}, bf16[4,64,128]{2,1,0:T(8,128)(2,1)S(1)}, u32[]{:S(2)}, u32[]{:S(2)}) collective-permute-start(bf16[4,64,128]{2,1,0:T(8,128)(2,1)S(1)} %get-tuple-element.16), channel_id=1, source_target_pairs={{4,0},{5,1},{6,2},{7,3},{0,4},{1,5},{2,6},{3,7},{12,8},{13,9},{14,... | collective-permute-start | bytes 196616 | tf_op jit(solution)/shard_map/ppermute | solution.py:13
  321.2 9.4 %collective-permute-start.14 = (bf16[4,64,128]{2,1,0:T(8,128)(2,1)S(1)}, bf16[4,64,128]{2,1,0:T(8,128)(2,1)S(1)}, u32[]{:S(2)}, u32[]{:S(2)}) collective-permute-start(bf16[4,64,128]{2,1,0:T(8,128)(2,1)S(1)} %get-tuple-element.17), channel_id=1, source_target_pairs={{5,0},{6,1},{7,2},{0,3},{1,4},{2,5},{3,6},{4,7},{13,8},{14,9},{15,... | collective-permute-start | bytes 196616 | tf_op jit(solution)/shard_map/ppermute | solution.py:13
  324.3 6.3 %collective-permute-start.13 = (bf16[4,64,128]{2,1,0:T(8,128)(2,1)S(1)}, bf16[4,64,128]{2,1,0:T(8,128)(2,1)S(1)}, u32[]{:S(2)}, u32[]{:S(2)}) collective-permute-start(bf16[4,64,128]{2,1,0:T(8,128)(2,1)S(1)} %get-tuple-element.18), channel_id=1, source_target_pairs={{6,0},{7,1},{0,2},{1,3},{2,4},{3,5},{4,6},{5,7},{14,8},{15,9},{8,1... | collective-permute-start | bytes 196616 | tf_op jit(solution)/shard_map/ppermute | solution.py:13
  360.1 6.1 %copy-start.2 = (f32[16,64,128]{2,1,0:T(8,128)S(1)}, f32[16,64,128]{2,1,0:T(8,128)}, u32[]{:S(2)}) copy-start(f32[16,64,128]{2,1,0:T(8,128)} %get-tuple-element.36) | copy-start | bytes 1572868
Sparse Core Ops, SparseCore 0:
  46.5 32.8 reduce-scatter.2
  154.8 23.6 all-gather.4
  220.3 32.9 reduce-scatter.4
  332.2 23.6 all-gather.6
where the time goes:
time: 375 us
  blocking collectives  137 us (37%)
  waiting for transfers between devices  127 us (34%)
  matrix products  28.7 us (8%)
  other arithmetic  23.6 us (6%)
  starting transfers between devices  21.9 us (6%)
  local copies, waits for them, and re-layouts  21.9 us (6%)
  between operations  14.2 us (4%)
    psum x2, blocking collectives, shards(): grad_sum = lax.psum(shaped, 'samp')  84.2 us
    reduce_scatter x2, waiting for transfers between devices, shards(): lax.psum_scatter(jnp.dot(dosage, values, preferred_element_type=jnp.float...  65.7 us
    all_gather x2, waiting for transfers between devices, shards(): gathered = lax.all_gather(held_rows[:, None], 'samp', axis=1, tiled=True)  43.2 us
    all_gather x2, blocking collectives, shards(): lax.all_gather(residual.astype(jnp.bfloat16), 'var', axis=0, tiled=True)  29.9 us
    all_gather x2, blocking collectives, shards(): lax.all_gather(local_rows[:, None], 'samp', axis=1, tiled=True)  22.8 us
    ppermute x16, starting transfers between devices, shifted(): return lax.ppermute(block, axis, route)  21.8 us
    ppermute x16, waiting for transfers between devices, shifted(): return lax.ppermute(block, axis, route)  18.3 us
    dot_general x2, matrix products, shards(): jnp.dot(dosage, values, preferred_element_type=jnp.float32) * inv_scale  14.7 us
  transfers between devices with their start and end apart: 20, of which 12 were waited for; matrix products, arithmetic and copies ran while one was open for 1% of the time, Pallas kernels for 0%

commit v1 on v0

--- a/solution.py
+++ b/solution.py
@@ -118,7 +118,11 @@
             * grad_scale
         )
         shaped = partial_grad.reshape(per_device, quarters, quarter_rows, right_cols)
-        grad_sum = lax.psum(shaped, "samp")
+        grad_sum = shaped
+        for hop in (1, 2):
+            grad_sum = grad_sum + lax.ppermute(
+                grad_sum, "samp", [(dev, dev ^ hop) for dev in range(4)]
+            )
         own_grad = lax.dynamic_index_in_dim(grad_sum, samp_index, 1, keepdims=False)
         outgoing = jnp.where(
             send_live[:, None, None], own_grad.astype(jnp.bfloat16)[send_unit], zero_half

time: 375 us -> 393 us (1.048)
  waiting for transfers between devices: 127 us -> 224 us
  blocking collectives: 137 us -> 52.8 us
  starting transfers between devices: 21.9 us -> 28 us
    ppermute x0 -> x4, waiting for transfers between devices: none -> 93.9 us  [shards(): lax.ppermute(grad_sum, 'samp', [(dev, dev ^ hop) for dev in range(4)])]
    psum x2 -> x0, blocking collectives: 84.2 us -> none  [shards(): grad_sum = lax.psum(shaped, 'samp')]
    ppermute x0 -> x4, starting transfers between devices: none -> 6.07 us  [shards(): lax.ppermute(grad_sum, 'samp', [(dev, dev ^ hop) for dev in range(4)])]
  transfers between devices with their start and end apart: 20 -> 24, of which waited for: 12 -> 16; matrix products, arithmetic and copies ran while one was open for 1% -> 1% of each run, Pallas kernels for 0% -> 0%
where the time goes in v1:
time: 393 us; the launch traced here: 392 us
  waiting for transfers between devices  224 us (57%)
  blocking collectives  52.8 us (13%)
  matrix products  28.6 us (7%)
  starting transfers between devices  28 us (7%)
  other arithmetic  24.1 us (6%)
  local copies, waits for them, and re-layouts  21 us (5%)
  between operations  14.2 us (4%)
    ppermute x4, waiting for transfers between devices, shards(): lax.ppermute(grad_sum, 'samp', [(dev, dev ^ hop) for dev in range(4)])  93.9 us
    reduce_scatter x2, waiting for transfers between devices, shards(): lax.psum_scatter(jnp.dot(dosage, values, preferred_element_type=jnp.float...  65.9 us
    all_gather x2, waiting for transfers between devices, shards(): gathered = lax.all_gather(held_rows[:, None], 'samp', axis=1, tiled=True)  45.4 us
    all_gather x2, blocking collectives, shards(): lax.all_gather(residual.astype(jnp.bfloat16), 'var', axis=0, tiled=True)  29.9 us
    all_gather x2, blocking collectives, shards(): lax.all_gather(local_rows[:, None], 'samp', axis=1, tiled=True)  22.9 us
    ppermute x16, starting transfers between devices, shifted(): return lax.ppermute(block, axis, route)  21.8 us
    ppermute x16, waiting for transfers between devices, shifted(): return lax.ppermute(block, axis, route)  18.3 us
    dot_general x2, matrix products, shards(): jnp.dot(dosage, values, preferred_element_type=jnp.float32) * inv_scale  14.7 us
  transfers between devices with their start and end apart: 24, of which 16 were waited for; matrix products, arithmetic and copies ran while one was open for 1% of the time, Pallas kernels for 0%

profile of v1, /device:TPU:0, one launch (start us, length us, event | category | flops | bytes accessed | tf_op | source)
XLA Modules:
  0.0 392.2 jit_solution(11516396567861290635)
XLA Ops:
  7.2 0.7 fusion.11
  8.0 0.7 broadcast_compare_fusion
  8.6 0.7 fusion.22
  9.4 0.6 reduce-window.12
  10.5 0.7 fusion.12
  11.2 0.6 gather_fusion
  11.8 0.8 select_reduce_fusion
  12.8 0.7 iota_subtract_fusion
  13.9 1.3 fusion.6
  15.2 0.6 gather_fusion.2
  15.9 4.6 %collective-permute-start = (bf16[4,64,128]{2,1,0:T(8,128)(2,1)S(1)}, bf16[4,64,128]{2,1,0:T(8,128)(2,1)S(1)}, u32[]{:S(2)}, u32[]{:S(2)}) collective-permute-start(bf16[4,64,128]{2,1,0:T(8,128)(2,1)S(1)} %get-tuple-element.27), channel_id=1, source_target_pairs={{1,0},{2,1},{3,2},{4,3},{5,4},{6,5},{7,6},{0,7},{9,8},{10,9},{11,1... | collective-permute-start | bytes 196616 | tf_op jit(solution)/shard_map/ppermute | solution.py:13
  20.5 3.3 collective-permute-start.1
  23.8 0.6 gather_fusion.1
  24.5 2.6 collective-permute-done.3
  27.7 11.3 %all-gather = bf16[8,256,128]{2,1,0:T(8,128)(2,1)S(1)} all-gather(bf16[8,64,128]{2,1,0:T(8,128)(2,1)S(1)} %gather_fusion.3), channel_id=2, replica_groups=mesh['samp'=4,'var'=8] {'samp'}, dimensions={1}, use_global_device_ids=true | all-gather | bytes 655360 | tf_op jit(solution)/shard_map/all_gather | solution.py:104
  39.0 7.4 %fusion.3 = f32[2048,128]{0,1:T(8,128)} fusion(bf16[2048,128]{1,0:T(8,128)(2,1)S(1)} %bitcast.108, bf16[2048,2048]{1,0:T(8,128)(2,1)} %param.8), kind=kOutput, calls=%fused_computation.21 | convolution fusion | flops 1074003968 | bytes 9961472 | tf_op jit(solution)/shard_map/dot_general | solution.py:107
  46.6 32.8 %reduce-scatter.3.cloned.1.call-done = f32[256,128]{0,1:T(8,128)} async-done(((f32[2048,128]{0,1:T(8,128)}), f32[256,128]{0,1:T(8,128)}) %reduce-scatter.3.cloned.1.call-update) | async-done | bytes 131088 | tf_op jit(solution)/shard_map/reduce_scatter | solution.py:106
  79.4 0.9 subtract_convert_fusion
  80.3 14.9 %all_gather.19 = bf16[2048,128]{0,1:T(8,128)(2,1)S(1)} all-gather(bf16[256,128]{0,1:T(8,128)(2,1)S(1)} %subtract_convert_fusion), channel_id=1, replica_groups=mesh['samp'=4,'var'=8] {'var'}, dimensions={0}, use_global_device_ids=true | all-gather | bytes 589824 | tf_op jit(solution)/shard_map/all_gather | solution.py:113
  95.3 4.7 %fusion.2 = f32[2048,128]{0,1:T(8,128)S(1)} fusion(bf16[2048,128]{0,1:T(8,128)(2,1)S(1)} %all_gather.19, bf16[2048,2048]{1,0:T(8,128)(2,1)} %param.8), kind=kOutput, calls=%fused_computation.19 | convolution fusion | flops 1074003968 | bytes 9961472 | tf_op jit(solution)/shard_map/dot_general | solution.py:115
  100.3 1.5 collective-permute-start.4
  101.8 24.0 %collective-permute-done.4 = f32[8,4,64,128]{3,2,1,0:T(8,128)S(1)} collective-permute-done((f32[8,4,64,128]{3,2,1,0:T(8,128)S(1)}, f32[8,4,64,128]{3,2,1,0:T(8,128)S(1)}, u32[]{:S(2)}, u32[]{:S(2)}) %collective-permute-start.4) | collective-permute-done | bytes 1048608 | tf_op jit(solution)/shard_map/ppermute | solution.py:123
  126.0 1.5 collective-permute-start.5
  127.7 22.9 %collective-permute-done.5 = f32[8,4,64,128]{3,2,1,0:T(8,128)S(1)} collective-permute-done((f32[8,4,64,128]{3,2,1,0:T(8,128)S(1)}, f32[8,4,64,128]{3,2,1,0:T(8,128)S(1)}, u32[]{:S(2)}, u32[]{:S(2)}) %collective-permute-start.5) | collective-permute-done | bytes 1048608 | tf_op jit(solution)/shard_map/ppermute | solution.py:123
  150.6 0.6 gather_fusion.4
  151.4 0.7 collective-permute-start.9
  152.1 3.1 collective-permute-start.8
  155.2 1.7 collective-permute-done.6
  157.0 4.5 %collective-permute-done.9 = bf16[4,64,128]{2,1,0:T(8,128)(2,1)S(1)} collective-permute-done((bf16[4,64,128]{2,1,0:T(8,128)(2,1)S(1)}, bf16[4,64,128]{2,1,0:T(8,128)(2,1)S(1)}, u32[]{:S(2)}, u32[]{:S(2)}) %collective-permute-start.9) | collective-permute-done | bytes 65568 | tf_op jit(solution)/shard_map/ppermute | solution.py:13
  161.6 0.6 gather_fusion.5
  162.2 0.8 bitcast_select_fusion.3
  163.4 3.2 reshape.362
  166.7 21.2 %all-gather.5.cloned.1.call-done = bf16[16,4,64,128]{3,2,1,0:T(8,128)(2,1)} async-done(((bf16[16,1,64,128]{3,2,1,0:T(8,128)(2,1)}), bf16[16,4,64,128]{3,2,1,0:T(8,128)(2,1)}) %all-gather.5.cloned.1.call-update) | async-done | bytes 1048592 | tf_op jit(solution)/shard_map/all_gather | solution.py:136
  188.0 4.2 %gather_fusion.6 = bf16[64,256,128]{2,1,0:T(8,128)(2,1)} fusion(bf16[16,256,128]{2,1,0:T(8,128)(2,1)} %bitcast.100, s32[1024]{0:T(1024)S(1)} %pad_clamp_fusion), kind=kCustom, calls=%fused_computation.6 | custom fusion | bytes 8388864 | tf_op jit(solution)/shard_map/gather | solution.py:138
  192.2 6.2 %bitcast_select_fusion.1 = bf16[16,1024,128]{2,1,0:T(8,128)(2,1)S(1)} fusion(pred[16,1024]{1,0:T(8,128)(4,1)S(1)} %bitcast.114, bf16[16,1024,128]{2,1,0:T(8,128)(2,1)} %bitcast.103), kind=kLoop, calls=%fused_computation.13 | loop fusion | flops 2097152 | bytes 8404992 | tf_op jit(solution)/shard_map/jit(_where)/select_n | solution.py:138
  198.4 1.8 fusion.38
  200.2 0.6 gather_fusion.7
  200.9 2.7 collective-permute-start.10
  203.8 3.3 collective-permute-start.11
  207.1 3.1 collective-permute-done.13
  210.2 0.6 gather_fusion.8
  210.8 11.6 %all-gather.1 = bf16[8,256,128]{2,1,0:T(8,128)(2,1)S(1)} all-gather(bf16[8,64,128]{2,1,0:T(8,128)(2,1)S(1)} %gather_fusion.8), channel_id=3, replica_groups=mesh['samp'=4,'var'=8] {'samp'}, dimensions={1}, use_global_device_ids=true | all-gather | bytes 655360 | tf_op jit(solution)/shard_map/all_gather | solution.py:104
  222.3 7.3 %fusion.1 = f32[2048,128]{0,1:T(8,128)} fusion(bf16[2048,128]{1,0:T(8,128)(2,1)S(1)} %bitcast.109, bf16[2048,2048]{1,0:T(8,128)(2,1)} %param.8), kind=kOutput, calls=%fused_computation.17 | convolution fusion | flops 1074003968 | bytes 9961472 | tf_op jit(solution)/shard_map/dot_general | solution.py:107
  229.7 33.1 %reduce-scatter.5.cloned.1.call-done = f32[256,128]{0,1:T(8,128)} async-done(((f32[2048,128]{0,1:T(8,128)}), f32[256,128]{0,1:T(8,128)}) %reduce-scatter.5.cloned.1.call-update) | async-done | bytes 131088 | tf_op jit(solution)/shard_map/reduce_scatter | solution.py:106
  262.8 0.9 fusion.33
  263.7 14.9 %all_gather.22 = bf16[2048,128]{0,1:T(8,128)(2,1)S(1)} all-gather(bf16[256,128]{0,1:T(8,128)(2,1)S(1)} %get-tuple-element.13), channel_id=1, replica_groups=mesh['samp'=4,'var'=8] {'var'}, dimensions={0}, use_global_device_ids=true | all-gather | bytes 589824 | tf_op jit(solution)/shard_map/all_gather | solution.py:113
  278.7 5.7 %fusion = f32[2048,128]{0,1:T(8,128)} fusion(bf16[2048,128]{0,1:T(8,128)(2,1)S(1)} %all_gather.22, bf16[2048,2048]{1,0:T(8,128)(2,1)} %param.8), kind=kOutput, calls=%fused_computation.15 | convolution fusion | flops 1074003968 | bytes 9961472 | tf_op jit(solution)/shard_map/dot_general | solution.py:115
  284.4 1.5 copy.27
  285.9 1.5 collective-permute-start.14
  287.5 23.9 %collective-permute-done.14 = f32[8,4,64,128]{3,2,1,0:T(8,128)S(1)} collective-permute-done((f32[8,4,64,128]{3,2,1,0:T(8,128)S(1)}, f32[8,4,64,128]{3,2,1,0:T(8,128)S(1)}, u32[]{:S(2)}, u32[]{:S(2)}) %collective-permute-start.14) | collective-permute-done | bytes 1048608 | tf_op jit(solution)/shard_map/ppermute | solution.py:123
  311.6 1.5 collective-permute-start.15
  313.1 23.1 %collective-permute-done.15 = f32[8,4,64,128]{3,2,1,0:T(8,128)S(1)} collective-permute-done((f32[8,4,64,128]{3,2,1,0:T(8,128)S(1)}, f32[8,4,64,128]{3,2,1,0:T(8,128)S(1)}, u32[]{:S(2)}, u32[]{:S(2)}) %collective-permute-start.15) | collective-permute-done | bytes 1048608 | tf_op jit(solution)/shard_map/ppermute | solution.py:123
  336.2 0.6 gather_fusion.9
  337.0 0.7 collective-permute-start.19
  337.7 3.1 collective-permute-start.18
  340.8 1.8 collective-permute-done.16
  342.6 4.5 %collective-permute-done.19 = bf16[4,64,128]{2,1,0:T(8,128)(2,1)S(1)} collective-permute-done((bf16[4,64,128]{2,1,0:T(8,128)(2,1)S(1)}, bf16[4,64,128]{2,1,0:T(8,128)(2,1)S(1)}, u32[]{:S(2)}, u32[]{:S(2)}) %collective-permute-start.19) | collective-permute-done | bytes 65568 | tf_op jit(solution)/shard_map/ppermute | solution.py:13
  347.2 0.6 gather_fusion.10
  347.8 0.8 bitcast_select_fusion.2
  348.6 0.8 copy.28
  349.4 24.1 %all-gather.7.cloned.1.call-done = bf16[16,4,64,128]{3,2,1,0:T(8,128)(2,1)} async-done(((bf16[16,1,64,128]{3,2,1,0:T(8,128)(2,1)}), bf16[16,4,64,128]{3,2,1,0:T(8,128)(2,1)}) %all-gather.7.cloned.1.call-update) | async-done | bytes 1048592 | tf_op jit(solution)/shard_map/all_gather | solution.py:136
  373.5 4.2 %gather_fusion.11 = bf16[64,256,128]{2,1,0:T(8,128)(2,1)} fusion(bf16[16,256,128]{2,1,0:T(8,128)(2,1)} %bitcast.101, s32[1024]{0:T(1024)S(1)} %pad_clamp_fusion), kind=kCustom, calls=%fused_computation.11 | custom fusion | bytes 8388864 | tf_op jit(solution)/shard_map/gather | solution.py:138
  377.7 6.1 %bitcast_select_fusion = bf16[16,1024,128]{2,1,0:T(8,128)(2,1)S(1)} fusion(pred[16,1024]{1,0:T(8,128)(4,1)S(1)} %bitcast.115, bf16[16,1024,128]{2,1,0:T(8,128)(2,1)} %bitcast.102), kind=kLoop, calls=%fused_computation.12 | loop fusion | flops 2097152 | bytes 8404992 | tf_op jit(solution)/shard_map/jit(_where)/select_n | solution.py:138
  383.9 1.8 multiply_select_fusion
  (86 shorter events, 4.4 us)
Async XLA Ops:
  7.2 72.2 %reduce-scatter.3.cloned.1.call-start = ((), (), s32[]{:S(2)}) async-start(), calls=%async_computation.2 | async-start | bytes 1179648 | tf_op jit(solution)/shard_map/reduce_scatter | solution.py:106
  15.9 8.6 %collective-permute-start = (bf16[4,64,128]{2,1,0:T(8,128)(2,1)S(1)}, bf16[4,64,128]{2,1,0:T(8,128)(2,1)S(1)}, u32[]{:S(2)}, u32[]{:S(2)}) collective-permute-start(bf16[4,64,128]{2,1,0:T(8,128)(2,1)S(1)} %get-tuple-element.27), channel_id=1, source_target_pairs={{1,0},{2,1},{3,2},{4,3},{5,4},{6,5},{7,6},{0,7},{9,8},{10,9},{11,1... | collective-permute-start | bytes 196616 | tf_op jit(solution)/shard_map/ppermute | solution.py:13
  20.5 6.6 %collective-permute-start.3 = (bf16[4,64,128]{2,1,0:T(8,128)(2,1)S(1)}, bf16[4,64,128]{2,1,0:T(8,128)(2,1)S(1)}, u32[]{:S(2)}, u32[]{:S(2)}) collective-permute-start(bf16[4,64,128]{2,1,0:T(8,128)(2,1)S(1)} %get-tuple-element.28), channel_id=1, source_target_pairs={{4,0},{5,1},{6,2},{7,3},{0,4},{1,5},{2,6},{3,7},{12,8},{13,9},{14,... | collective-permute-start | bytes 196616 | tf_op jit(solution)/shard_map/ppermute | solution.py:13
  20.5 6.6 %collective-permute-start.2 = (bf16[4,64,128]{2,1,0:T(8,128)(2,1)S(1)}, bf16[4,64,128]{2,1,0:T(8,128)(2,1)S(1)}, u32[]{:S(2)}, u32[]{:S(2)}) collective-permute-start(bf16[4,64,128]{2,1,0:T(8,128)(2,1)S(1)} %get-tuple-element.29), channel_id=1, source_target_pairs={{3,0},{4,1},{5,2},{6,3},{7,4},{0,5},{1,6},{2,7},{11,8},{12,9},{13,... | collective-permute-start | bytes 196616 | tf_op jit(solution)/shard_map/ppermute | solution.py:13
  20.5 6.6 %collective-permute-start.1 = (bf16[4,64,128]{2,1,0:T(8,128)(2,1)S(1)}, bf16[4,64,128]{2,1,0:T(8,128)(2,1)S(1)}, u32[]{:S(2)}, u32[]{:S(2)}) collective-permute-start(bf16[4,64,128]{2,1,0:T(8,128)(2,1)S(1)} %get-tuple-element.30), channel_id=1, source_target_pairs={{2,0},{3,1},{4,2},{5,3},{6,4},{7,5},{0,6},{1,7},{10,8},{11,9},{12,... | collective-permute-start | bytes 196616 | tf_op jit(solution)/shard_map/ppermute | solution.py:13
  39.0 7.4 %copy-start.3 = (f32[256,128]{1,0:T(8,128)S(1)}, f32[256,128]{1,0:T(8,128)}, u32[]{:S(2)}) copy-start(f32[256,128]{1,0:T(8,128)} %param.9) | copy-start | bytes 393220
  46.4 141.6 %all-gather.5.cloned.1.call-start = ((), (), s32[]{:S(2)}) async-start(), calls=%async_computation.3 | async-start | bytes 1310720 | tf_op jit(solution)/shard_map/all_gather | solution.py:136
  100.3 25.5 %collective-permute-start.4 = (f32[8,4,64,128]{3,2,1,0:T(8,128)S(1)}, f32[8,4,64,128]{3,2,1,0:T(8,128)S(1)}, u32[]{:S(2)}, u32[]{:S(2)}) collective-permute-start(f32[8,4,64,128]{3,2,1,0:T(8,128)S(1)} %bitcast.104), channel_id=1, source_target_pairs={{0,8},{8,0},{16,24},{24,16},{1,9},{9,1},{17,25},{25,17},{2,10},{10... | collective-permute-start | bytes 3145736 | tf_op jit(solution)/shard_map/ppermute | solution.py:123
  126.0 24.6 %collective-permute-start.5 = (f32[8,4,64,128]{3,2,1,0:T(8,128)S(1)}, f32[8,4,64,128]{3,2,1,0:T(8,128)S(1)}, u32[]{:S(2)}, u32[]{:S(2)}) collective-permute-start(f32[8,4,64,128]{3,2,1,0:T(8,128)S(1)} %add.161), channel_id=1, source_target_pairs={{0,16},{8,24},{16,0},{24,8},{1,17},{9,25},{17,1},{25,9},{2,18},{10... | collective-permute-start | bytes 3145736 | tf_op jit(solution)/shard_map/ppermute | solution.py:123
  151.3 5.6 %collective-permute-start.6 = (bf16[4,64,128]{2,1,0:T(8,128)(2,1)S(1)}, bf16[4,64,128]{2,1,0:T(8,128)(2,1)S(1)}, u32[]{:S(2)}, u32[]{:S(2)}) collective-permute-start(bf16[4,64,128]{2,1,0:T(8,128)(2,1)S(1)} %get-tuple-element.23), channel_id=1, source_target_pairs={{7,0},{0,1},{1,2},{2,3},{3,4},{4,5},{5,6},{6,7},{15,8},{8,9},{9,10... | collective-permute-start | bytes 196616 | tf_op jit(solution)/shard_map/ppermute | solution.py:13
  151.4 10.1 %collective-permute-start.9 = (bf16[4,64,128]{2,1,0:T(8,128)(2,1)S(1)}, bf16[4,64,128]{2,1,0:T(8,128)(2,1)S(1)}, u32[]{:S(2)}, u32[]{:S(2)}) collective-permute-start(bf16[4,64,128]{2,1,0:T(8,128)(2,1)S(1)} %get-tuple-element.24), channel_id=1, source_target_pairs={{4,0},{5,1},{6,2},{7,3},{0,4},{1,5},{2,6},{3,7},{12,8},{13,9},{14,... | collective-permute-start | bytes 196616 | tf_op jit(solution)/shard_map/ppermute | solution.py:13
  152.1 9.4 %collective-permute-start.8 = (bf16[4,64,128]{2,1,0:T(8,128)(2,1)S(1)}, bf16[4,64,128]{2,1,0:T(8,128)(2,1)S(1)}, u32[]{:S(2)}, u32[]{:S(2)}) collective-permute-start(bf16[4,64,128]{2,1,0:T(8,128)(2,1)S(1)} %get-tuple-element.25), channel_id=1, source_target_pairs={{5,0},{6,1},{7,2},{0,3},{1,4},{2,5},{3,6},{4,7},{13,8},{14,9},{15,... | collective-permute-start | bytes 196616 | tf_op jit(solution)/shard_map/ppermute | solution.py:13
  155.2 6.3 %collective-permute-start.7 = (bf16[4,64,128]{2,1,0:T(8,128)(2,1)S(1)}, bf16[4,64,128]{2,1,0:T(8,128)(2,1)S(1)}, u32[]{:S(2)}, u32[]{:S(2)}) collective-permute-start(bf16[4,64,128]{2,1,0:T(8,128)(2,1)S(1)} %get-tuple-element.26), channel_id=1, source_target_pairs={{6,0},{7,1},{0,2},{1,3},{2,4},{3,5},{4,6},{5,7},{14,8},{15,9},{8,1... | collective-permute-start | bytes 196616 | tf_op jit(solution)/shard_map/ppermute | solution.py:13
  163.0 99.8 %reduce-scatter.5.cloned.1.call-start = ((), (), s32[]{:S(2)}) async-start(), calls=%async_computation.4 | async-start | bytes 1179648 | tf_op jit(solution)/shard_map/reduce_scatter | solution.py:106
  192.2 6.2 %copy-start = (f32[16,64,128]{2,1,0:T(8,128)S(1)}, f32[16,64,128]{2,1,0:T(8,128)}, u32[]{:S(2)}) copy-start(f32[16,64,128]{2,1,0:T(8,128)} %param.10) | copy-start | bytes 1572868
  192.2 6.2 %copy-start.1 = (f32[16,64,128]{2,1,0:T(8,128)S(1)}, f32[16,64,128]{2,1,0:T(8,128)}, u32[]{:S(2)}) copy-start(f32[16,64,128]{2,1,0:T(8,128)} %param.11) | copy-start | bytes 1572868
  192.2 6.2 %copy-start.4 = (f32[128]{0:T(128)S(1)}, f32[128]{0:T(128)}, u32[]{:S(2)}) copy-start(f32[128]{0:T(128)} %param.13) | copy-start | bytes 1540
  200.9 6.2 %collective-permute-start.10 = (bf16[4,64,128]{2,1,0:T(8,128)(2,1)S(1)}, bf16[4,64,128]{2,1,0:T(8,128)(2,1)S(1)}, u32[]{:S(2)}, u32[]{:S(2)}) collective-permute-start(bf16[4,64,128]{2,1,0:T(8,128)(2,1)S(1)} %get-tuple-element.19), channel_id=1, source_target_pairs={{1,0},{2,1},{3,2},{4,3},{5,4},{6,5},{7,6},{0,7},{9,8},{10,9},{11,1... | collective-permute-start | bytes 196616 | tf_op jit(solution)/shard_map/ppermute | solution.py:13
  203.6 6.6 %collective-permute-start.13 = (bf16[4,64,128]{2,1,0:T(8,128)(2,1)S(1)}, bf16[4,64,128]{2,1,0:T(8,128)(2,1)S(1)}, u32[]{:S(2)}, u32[]{:S(2)}) collective-permute-start(bf16[4,64,128]{2,1,0:T(8,128)(2,1)S(1)} %get-tuple-element.20), channel_id=1, source_target_pairs={{4,0},{5,1},{6,2},{7,3},{0,4},{1,5},{2,6},{3,7},{12,8},{13,9},{14,... | collective-permute-start | bytes 196616 | tf_op jit(solution)/shard_map/ppermute | solution.py:13
  203.6 6.6 %collective-permute-start.12 = (bf16[4,64,128]{2,1,0:T(8,128)(2,1)S(1)}, bf16[4,64,128]{2,1,0:T(8,128)(2,1)S(1)}, u32[]{:S(2)}, u32[]{:S(2)}) collective-permute-start(bf16[4,64,128]{2,1,0:T(8,128)(2,1)S(1)} %get-tuple-element.21), channel_id=1, source_target_pairs={{3,0},{4,1},{5,2},{6,3},{7,4},{0,5},{1,6},{2,7},{11,8},{12,9},{13,... | collective-permute-start | bytes 196616 | tf_op jit(solution)/shard_map/ppermute | solution.py:13
  203.8 6.4 %collective-permute-start.11 = (bf16[4,64,128]{2,1,0:T(8,128)(2,1)S(1)}, bf16[4,64,128]{2,1,0:T(8,128)(2,1)S(1)}, u32[]{:S(2)}, u32[]{:S(2)}) collective-permute-start(bf16[4,64,128]{2,1,0:T(8,128)(2,1)S(1)} %get-tuple-element.22), channel_id=1, source_target_pairs={{2,0},{3,1},{4,2},{5,3},{6,4},{7,5},{0,6},{1,7},{10,8},{11,9},{12,... | collective-permute-start | bytes 196616 | tf_op jit(solution)/shard_map/ppermute | solution.py:13
  229.7 143.8 %all-gather.7.cloned.1.call-start = ((), (), s32[]{:S(2)}) async-start(), calls=%async_computation.5 | async-start | bytes 1310720 | tf_op jit(solution)/shard_map/all_gather | solution.py:136
  285.9 25.5 %collective-permute-start.14 = (f32[8,4,64,128]{3,2,1,0:T(8,128)S(1)}, f32[8,4,64,128]{3,2,1,0:T(8,128)S(1)}, u32[]{:S(2)}, u32[]{:S(2)}) collective-permute-start(f32[8,4,64,128]{3,2,1,0:T(8,128)S(1)} %bitcast.106), channel_id=1, source_target_pairs={{0,8},{8,0},{16,24},{24,16},{1,9},{9,1},{17,25},{25,17},{2,10},{10... | collective-permute-start | bytes 3145736 | tf_op jit(solution)/shard_map/ppermute | solution.py:123
  311.6 24.6 %collective-permute-start.15 = (f32[8,4,64,128]{3,2,1,0:T(8,128)S(1)}, f32[8,4,64,128]{3,2,1,0:T(8,128)S(1)}, u32[]{:S(2)}, u32[]{:S(2)}) collective-permute-start(f32[8,4,64,128]{3,2,1,0:T(8,128)S(1)} %add.170), channel_id=1, source_target_pairs={{0,16},{8,24},{16,0},{24,8},{1,17},{9,25},{17,1},{25,9},{2,18},{10... | collective-permute-start | bytes 3145736 | tf_op jit(solution)/shard_map/ppermute | solution.py:123
  337.0 5.6 %collective-permute-start.16 = (bf16[4,64,128]{2,1,0:T(8,128)(2,1)S(1)}, bf16[4,64,128]{2,1,0:T(8,128)(2,1)S(1)}, u32[]{:S(2)}, u32[]{:S(2)}) collective-permute-start(bf16[4,64,128]{2,1,0:T(8,128)(2,1)S(1)} %get-tuple-element.15), channel_id=1, source_target_pairs={{7,0},{0,1},{1,2},{2,3},{3,4},{4,5},{5,6},{6,7},{15,8},{8,9},{9,10... | collective-permute-start | bytes 196616 | tf_op jit(solution)/shard_map/ppermute | solution.py:13
  337.0 10.1 %collective-permute-start.19 = (bf16[4,64,128]{2,1,0:T(8,128)(2,1)S(1)}, bf16[4,64,128]{2,1,0:T(8,128)(2,1)S(1)}, u32[]{:S(2)}, u32[]{:S(2)}) collective-permute-start(bf16[4,64,128]{2,1,0:T(8,128)(2,1)S(1)} %get-tuple-element.16), channel_id=1, source_target_pairs={{4,0},{5,1},{6,2},{7,3},{0,4},{1,5},{2,6},{3,7},{12,8},{13,9},{14,... | collective-permute-start | bytes 196616 | tf_op jit(solution)/shard_map/ppermute | solution.py:13
  337.7 9.4 %collective-permute-start.18 = (bf16[4,64,128]{2,1,0:T(8,128)(2,1)S(1)}, bf16[4,64,128]{2,1,0:T(8,128)(2,1)S(1)}, u32[]{:S(2)}, u32[]{:S(2)}) collective-permute-start(bf16[4,64,128]{2,1,0:T(8,128)(2,1)S(1)} %get-tuple-element.17), channel_id=1, source_target_pairs={{5,0},{6,1},{7,2},{0,3},{1,4},{2,5},{3,6},{4,7},{13,8},{14,9},{15,... | collective-permute-start | bytes 196616 | tf_op jit(solution)/shard_map/ppermute | solution.py:13
  340.8 6.3 %collective-permute-start.17 = (bf16[4,64,128]{2,1,0:T(8,128)(2,1)S(1)}, bf16[4,64,128]{2,1,0:T(8,128)(2,1)S(1)}, u32[]{:S(2)}, u32[]{:S(2)}) collective-permute-start(bf16[4,64,128]{2,1,0:T(8,128)(2,1)S(1)} %get-tuple-element.18), channel_id=1, source_target_pairs={{6,0},{7,1},{0,2},{1,3},{2,4},{3,5},{4,6},{5,7},{14,8},{15,9},{8,1... | collective-permute-start | bytes 196616 | tf_op jit(solution)/shard_map/ppermute | solution.py:13
  377.7 6.1 %copy-start.2 = (f32[16,64,128]{2,1,0:T(8,128)S(1)}, f32[16,64,128]{2,1,0:T(8,128)}, u32[]{:S(2)}) copy-start(f32[16,64,128]{2,1,0:T(8,128)} %get-tuple-element.36) | copy-start | bytes 1572868
Sparse Core Ops, SparseCore 0:
  46.5 32.8 reduce-scatter.2
  163.1 24.7 all-gather.4
  229.8 32.9 reduce-scatter.4
  348.8 24.7 all-gather.6
